TPU v7x, 32 devices: a whole 2x2x4 slice. The times are simulated.
32 devices in a mesh: strip: 4 (over z), cross: 8 (over y, x, core).
Axes of the slice: x: 2, y: 2, z: 4, core: 2. Of those that a mesh axis runs over, the one named last changes fastest.
Arguments:
- rhs: bfloat16 [4, 64, 14336], P('strip', None, 'cross'), may hold values from -6 to 6
- inverse: bfloat16 [4, 8, 1792, 1792], P('strip', 'cross'), may hold values from -2 to 2
- dis_fwd: bfloat16 [4, 8, 256, 1792], P('strip', 'cross'), may hold values from -0.1875 to 0.1875
- agg_fwd: bfloat16 [4, 14336, 256], P('strip', 'cross'), may hold values from -0.0625 to 0.0625
- phase_fwd: float32 [4, 128], P('strip'), may hold values from -3.140625 to 3.140625
- gain_fwd: float32 [4, 128], P('strip'), may hold values from 0.5 to 1
- dis_back: bfloat16 [4, 8, 256, 1792], P('strip', 'cross'), may hold values from -0.1875 to 0.1875
- agg_back: bfloat16 [4, 14336, 256], P('strip', 'cross'), may hold values from -0.0625 to 0.0625
- phase_back: float32 [4, 128], P('strip'), may hold values from -3.140625 to 3.140625
- gain_back: float32 [4, 128], P('strip'), may hold values from 0.5 to 1
Outputs:
- first_pass: float32 [4, 64, 14336], P('strip', None, 'cross')
- solution: float32 [4, 64, 14336], P('strip', None, 'cross')
All inputs are finite; a program needn't handle non-finite values.
Results may differ from a plain program's by a relative error of at most 0.04.
Values may be sent and summed in bfloat16 or wider, within the bound.
A program may use at most 64 MiB of HBM per device.

v0:
```python
import functools

import jax
import jax.numpy as jnp
from jax import lax
from jax.experimental import pallas as pl
from jax.experimental.pallas import tpu as pltpu
from jax.sharding import PartitionSpec as P

MESH = pl.DeviceIdType.MESH
BF = jnp.bfloat16
F32 = jnp.float32
KINDS = 11
T_RS, B_RS, T_AG, N_RS, N_AG, E_RS, C_IN, C_ON, C_SH, D_ON, D_SH = range(KINDS)


def dot(a, b):
    return jnp.dot(a, b, preferred_element_type=F32)


def kernel(
    strips, n, width,
    rhs, inverse, dis_fwd, agg_fwd, phase_fwd, gain_fwd, dis_back, agg_back, phase_back, gain_back,
    first_ref, second_ref,
    x_f, x_b, inv, agg_f, agg_b, p, u_f, u_b,
    t_own, t_out, t_in, n_own, n_out, n_in, t_all, n_all,
    b_own, b_out, b_in, e_own, e_out, e_in, c_in, b_red, e_red,
    c_out, c_all, d_out, d_all,
    turns, coef, load_sem, sems,
):
    s = lax.axis_index("strip")
    me = lax.axis_index("cross")
    is_first = s == 0
    is_last = s == strips - 1
    inner = jnp.logical_and(s > 0, s < strips - 1)
    angles = rhs.shape[1]
    modes = agg_f.shape[1]
    half = modes // 2
    unk = p.shape[1]
    blocks = unk // width
    rows = angles // n

    load_rhs = pltpu.make_async_copy(rhs.at[0], x_b.at[pl.ds(0, angles)], load_sem.at[0])
    load_dis = pltpu.make_async_copy(dis_fwd.at[0, 0], x_f, load_sem.at[1])
    load_agg = pltpu.make_async_copy(agg_fwd.at[0], agg_f, load_sem.at[2])
    load_last = pltpu.make_async_copy(agg_back.at[0], agg_f, load_sem.at[2])
    load_dis_b = pltpu.make_async_copy(
        dis_back.at[0, 0], x_b.at[pl.ds(angles, modes)], load_sem.at[3]
    )
    load_agg_b = pltpu.make_async_copy(agg_back.at[0], agg_b, load_sem.at[4])
    inv_loads = [
        pltpu.make_async_copy(
            inverse.at[0, 0, :, pl.ds(j * width, width)], inv.at[j], load_sem.at[5 + j]
        )
        for j in range(blocks)
    ]
    turn_loads = [
        pltpu.make_async_copy(ref, turns.at[j], load_sem.at[5 + blocks + j])
        for j, ref in enumerate((phase_fwd, gain_fwd, phase_back, gain_back))
    ]
    @pl.when(is_first)
    def _():
        load_rhs.start()

    @pl.when(s > 0)
    def _():
        load_dis.start()

    @pl.when(is_last)
    def _():
        load_last.start()

    @pl.when(s < strips - 1)
    def _():
        load_agg.start()

    for copy in inv_loads:
        copy.start()

    @pl.when(s > 0)
    def _():
        load_rhs.start()

    @pl.when(s < strips - 1)
    def _():
        load_dis_b.start()

    @pl.when(inner)
    def _():
        load_agg_b.start()

    for copy in turn_loads:
        copy.start()

    barrier = pltpu.get_barrier_semaphore()

    def greet(strip, peer):
        pl.semaphore_signal(barrier, inc=1, device_id=(strip, peer), device_id_type=MESH)

    def others(fn):
        def step(j, carry):
            fn(lax.rem(me + j, n))
            return carry
        lax.fori_loop(1, n, step, 0)

    def everyone(fn):
        def step(j, carry):
            fn(lax.rem(me + j, n))
            return carry
        lax.fori_loop(0, n, step, 0)

    others(lambda peer: greet(s, peer))

    @pl.when(s > 0)
    def _():
        everyone(lambda peer: greet(s - 1, peer))

    @pl.when(s < strips - 1)
    def _():
        everyone(lambda peer: greet(s + 1, peer))

    def remote(kind, src, dst, strip, peer):
        return pltpu.make_async_remote_copy(
            src_ref=src,
            dst_ref=dst,
            send_sem=sems.at[kind, 0, peer],
            recv_sem=sems.at[kind, 1, me],
            device_id=(strip, peer),
            device_id_type=MESH,
        )

    def arrived(kind, dst, peer):
        pltpu.make_async_remote_copy(
            src_ref=dst.at[peer],
            dst_ref=dst.at[peer],
            send_sem=sems.at[kind, 0, peer],
            recv_sem=sems.at[kind, 1, peer],
            device_id=(s, peer),
            device_id_type=MESH,
        ).wait_recv()

    def scatter(kind, out, into):
        others(lambda peer: remote(kind, out.at[peer], into.at[me], s, peer).start())

    def scatter_sent(kind, out, into):
        others(lambda peer: remote(kind, out.at[peer], into.at[me], s, peer).wait_send())

    def total(kind, own, into):
        others(lambda peer: arrived(kind, into, peer))
        value = own[me]
        for j in range(1, n):
            value = value + into[lax.rem(me + j, n)].astype(F32)
        return value

    def share(kind, buf):
        others(lambda peer: remote(kind, buf.at[me], buf.at[me], s, peer).start())

    def share_sent(kind, buf):
        others(lambda peer: remote(kind, buf.at[me], buf.at[me], s, peer).wait_send())

    def split(value, own, out):
        part = value.shape[0] // n
        for k in range(n):
            piece = value[k * part:(k + 1) * part]
            own[k] = piece
            out[k] = piece.astype(BF)

    def joined(buf):
        return jnp.concatenate([buf[k] for k in range(n)], axis=0)

    def rotated(value, at):
        real, imag = value[:, :half], value[:, half:]
        cosine, sine = coef[at], coef[at + 1]
        return jnp.concatenate(
            [cosine * real - sine * imag, sine * real + cosine * imag], axis=1
        )

    def columns(j):
        return slice(j * width, (j + 1) * width)

    load_agg.wait()

    @pl.when(is_first)
    def _():
        load_rhs.wait()
        value = None
        for j in range(blocks):
            inv_loads[j].wait()
            product = dot(x_b[:angles], inv[j])
            p[:, columns(j)] = product
            term = dot(product.astype(BF), agg_f[columns(j)])
            value = term if value is None else value + term
        split(value, b_own, b_out)

    @pl.when(s > 0)
    def _():
        load_dis.wait()
        for j in range(blocks):
            inv_loads[j].wait()
            product = dot(x_f[...], inv[j]).astype(BF)
            u_f[:, columns(j)] = product
            term = dot(product, agg_f[columns(j)]).reshape(t_own.shape)
            if j == 0:
                t_own[...] = term
            else:
                t_own[...] += term
        t_out[...] = t_own[...].astype(BF)

    greeted = (n - 1) + jnp.where(s > 0, n, 0) + jnp.where(s < strips - 1, n, 0)
    pl.semaphore_wait(barrier, greeted)

    @pl.when(is_first)
    def _():
        everyone(lambda peer: remote(C_IN, b_out.at[peer], c_in.at[me], s + 1, peer).start())

    @pl.when(s > 0)
    def _():
        scatter(T_RS, t_out, t_in)
        load_rhs.wait()
        value = None
        for j in range(blocks):
            product = dot(x_b[:angles], inv[j])
            p[:, columns(j)] = product
            term = dot(product.astype(BF), agg_f[columns(j)])
            value = term if value is None else value + term
        split(value, b_own, b_out)
        scatter(B_RS, b_out, b_in)

    for copy in turn_loads:
        copy.wait()
    for at in (0, 2):
        coef[at] = jnp.cos(turns[at]) * turns[at + 1]
        coef[at + 1] = jnp.sin(turns[at]) * turns[at + 1]

    @pl.when(is_first)
    def _():
        load_dis_b.wait()
        for j in range(blocks):
            u_b[:, columns(j)] = dot(x_b[angles:], inv[j]).astype(BF)

    @pl.when(s > 0)
    def _():
        t_all[me] = total(T_RS, t_own, t_in).astype(BF)
        share(T_AG, t_all)

    @pl.when(inner)
    def _():
        load_dis_b.wait()
        load_agg_b.wait()
        for j in range(blocks):
            product = dot(x_b[angles:], inv[j]).astype(BF)
            u_b[:, columns(j)] = product
            term = dot(product, agg_b[columns(j)]).reshape(n_own.shape)
            if j == 0:
                n_own[...] = term
            else:
                n_own[...] += term
        n_out[...] = n_own[...].astype(BF)

    @pl.when(s > 0)
    def _():
        b_red[...] = total(B_RS, b_own, b_in)

    @pl.when(inner)
    def _():
        scatter(N_RS, n_out, n_in)

    def take_carry():
        @pl.when(s == 1)
        def _():
            everyone(lambda peer: arrived(C_IN, c_in, peer))
            value = c_in[0].astype(F32)
            for j in range(1, n):
                value = value + c_in[j].astype(F32)
            c_all[me] = value.astype(BF)

        @pl.when(s > 1)
        def _():
            arrived(C_ON, c_all, me)

    @pl.when(inner)
    def _():
        others(lambda peer: arrived(T_AG, t_all, peer))
        matrix = joined(t_all)
        take_carry()
        held = c_all[me]
        leaving = rotated(held.astype(F32), 0) + b_red[...]
        c_out[...] = (leaving - dot(held, matrix)).astype(BF)
        remote(C_ON, c_out, c_all.at[me], s + 1, me).start()
        share(C_SH, c_all)

    @pl.when(inner)
    def _():
        n_all[me] = total(N_RS, n_own, n_in).astype(BF)
        share(N_AG, n_all)

    @pl.when(is_last)
    def _():
        others(lambda peer: arrived(T_AG, t_all, peer))
        matrix = joined(t_all)
        take_carry()
        d_out[...] = (b_red[...] - dot(c_all[me], matrix)).astype(BF)

    def send_back():
        @pl.when(s == 1)
        def _():
            everyone(lambda peer: remote(D_ON, d_out, d_all.at[me], s - 1, peer).start())

        @pl.when(s > 1)
        def _():
            remote(D_ON, d_out, d_all.at[me], s - 1, me).start()

    @pl.when(is_last)
    def _():
        send_back()
        share(C_SH, c_all)

    @pl.when(is_first)
    def _():
        first_ref[0] = p[...]

    @pl.when(s > 0)
    def _():
        others(lambda peer: arrived(C_SH, c_all, peer))
        first_ref[0] = p[...] - dot(joined(c_all), u_f[...])

    @pl.when(inner)
    def _():
        split(dot(first_ref[0].astype(BF), agg_b[...]), e_own, e_out)
        scatter(E_RS, e_out, e_in)
        others(lambda peer: arrived(N_AG, n_all, peer))
        e_red[...] = total(E_RS, e_own, e_in)
        matrix = joined(n_all)
        arrived(D_ON, d_all, me)
        held = d_all[me]
        leaving = rotated(held.astype(F32), 2) + e_red[...]
        d_out[...] = (leaving - dot(held, matrix)).astype(BF)
        send_back()
        share(D_SH, d_all)

    @pl.when(is_last)
    def _():
        second_ref[0] = first_ref[0]

    @pl.when(is_first)
    def _():
        everyone(lambda peer: arrived(D_ON, d_all, peer))

    @pl.when(inner)
    def _():
        others(lambda peer: arrived(D_SH, d_all, peer))

    @pl.when(s < strips - 1)
    def _():
        second_ref[0] = first_ref[0] - dot(joined(d_all), u_b[...])

    @pl.when(is_first)
    def _():
        everyone(lambda peer: remote(C_IN, b_out.at[peer], c_in.at[me], s + 1, peer).wait_send())

    @pl.when(inner)
    def _():
        scatter_sent(N_RS, n_out, n_in)
        share_sent(N_AG, n_all)
        scatter_sent(E_RS, e_out, e_in)
        remote(C_ON, c_out, c_all.at[me], s + 1, me).wait_send()
        share_sent(D_SH, d_all)

    @pl.when(s > 0)
    def _():
        scatter_sent(T_RS, t_out, t_in)
        share_sent(T_AG, t_all)
        scatter_sent(B_RS, b_out, b_in)
        share_sent(C_SH, c_all)

    @pl.when(s == 1)
    def _():
        everyone(lambda peer: remote(D_ON, d_out, d_all.at[me], s - 1, peer).wait_send())

    @pl.when(s > 1)
    def _():
        remote(D_ON, d_out, d_all.at[me], s - 1, me).wait_send()


def body(strips, n, rhs, inverse, dis_fwd, agg_fwd, phase_fwd, gain_fwd, dis_back, agg_back, phase_back, gain_back):
    _, angles, unk = rhs.shape
    modes = agg_fwd.shape[2]
    width = 256 if unk % 256 == 0 else unk
    blocks = unk // width
    rows, part = angles // n, modes // n
    hbm = pl.BlockSpec(memory_space=pl.ANY)
    vmem = pl.BlockSpec(memory_space=pltpu.VMEM)
    out = pltpu.VMEM((1, angles, unk), F32)
    return pl.pallas_call(
        functools.partial(kernel, strips, n, width),
        out_shape=(out, out),
        in_specs=[hbm] * 10,
        out_specs=(vmem, vmem),
        scratch_shapes=[
            pltpu.VMEM((modes, unk), BF),
            pltpu.VMEM((angles + modes, unk), BF),
            pltpu.VMEM((blocks, unk, width), BF),
            pltpu.VMEM((unk, modes), BF),
            pltpu.VMEM((unk, modes), BF),
            pltpu.VMEM((angles, unk), F32),
            pltpu.VMEM((modes, unk), BF),
            pltpu.VMEM((modes, unk), BF),
        ]
        + [pltpu.VMEM((n, part, modes), kind) for kind in (F32, BF, BF) * 2 + (BF, BF)]
        + [pltpu.VMEM((n, rows, modes), kind) for kind in (F32, BF, BF) * 2 + (BF,)]
        + [pltpu.VMEM((rows, modes), F32)] * 2
        + [pltpu.VMEM((rows, modes), BF), pltpu.VMEM((n, rows, modes), BF)] * 2
        + [pltpu.VMEM((4, 1, modes // 2), F32)] * 2
        + [pltpu.SemaphoreType.DMA((9 + blocks,)), pltpu.SemaphoreType.DMA((KINDS, 2, n))],
        compiler_params=pltpu.CompilerParams(
            collective_id=0, has_side_effects=True, vmem_limit_bytes=60 * 1024 * 1024
        ),
    )(rhs, inverse, dis_fwd, agg_fwd, phase_fwd, gain_fwd, dis_back, agg_back, phase_back, gain_back)


def solution(mesh):
    strips, n = mesh.shape["strip"], mesh.shape["cross"]
    return jax.shard_map(
        functools.partial(body, strips, n),
        mesh=mesh,
        in_specs=(
            P("strip", None, "cross"),
            P("strip", "cross", None, None),
            P("strip", "cross", None, None),
            P("strip", "cross", None),
            P("strip", None),
            P("strip", None),
            P("strip", "cross", None, None),
            P("strip", "cross", None),
            P("strip", None),
            P("strip", None),
        ),
        out_specs=(P("strip", None, "cross"), P("strip", None, "cross")),
        check_vma=False,
    )
```

profile of v0, /device:TPU:0, one launch (start us, length us, event | category | flops | bytes accessed | tf_op | source)
XLA Modules:
  0.0 36.8 jit_solution(3304614114125858924)
XLA Ops:
  0.6 34.6 %shard_map.113 = (f32[1,64,1792]{2,1,0:T(8,128)S(1)}, f32[1,64,1792]{2,1,0:T(8,128)S(1)}) custom-call(bf16[1,64,1792]{2,1,0:T(8,128)(2,1)} %rhs.1, bf16[1,1,1792,1792]{3,2,1,0:T(8,128)(2,1)} %inverse.1, bf16[1,1,256,1792]{3,2,1,0:T(8,128)(2,1)} %dis_fwd.1, bf16[1,1792,256]{2,1,0:T(8,128)(2,1)} %agg_fwd.1, f32[1,128]{1,0:T(1,128)} %phase_fwd.1, ...), custom_call_target="tpu_custom_call" | custom-call | tf_op jit(solution)/shard_map/pallas_call | solution.py:394
  35.2 0.8 %copy.14 = f32[1,64,1792]{2,1,0:T(8,128)} copy(f32[1,64,1792]{2,1,0:T(8,128)S(1)} %get-tuple-element.2) | data formatting | bytes 917504
  36.0 0.8 %copy.15 = f32[1,64,1792]{2,1,0:T(8,128)} copy(f32[1,64,1792]{2,1,0:T(8,128)S(1)} %get-tuple-element.3) | data formatting | bytes 917504
where the time goes:
time: 36.9 us; the launch traced here: 36.8 us
  Pallas kernels  34.6 us (94%)
  local copies, waits for them, and re-layouts  1.54 us (4%)
  between operations  0.64 us (2%)
    pallas_call x1, Pallas kernels, body(): pl.pallas_call(functools.partial(kernel, strips, n, width), out_shape=(ou...  34.6 us
    unnamed x2, local copies, waits for them, and re-layouts  1.54 us

commit v1 on v0

v1 whole, which is shorter than its diff:
```python
import functools

import jax
import jax.numpy as jnp
from jax import lax
from jax.experimental import pallas as pl
from jax.experimental.pallas import tpu as pltpu
from jax.sharding import PartitionSpec as P

MESH = pl.DeviceIdType.MESH
BF = jnp.bfloat16
F32 = jnp.float32
KINDS = 16
(
    T_RS, T_AG, M_RS, M_AG, N_RS, N_AG, L_RS, L_AG,
    B_RS, Q_RS, R_RS, C_IN, C_ON, C_SH, D_ON, D_SH,
) = range(KINDS)


def dot(a, b):
    return jnp.dot(a, b, preferred_element_type=F32)


def kernel(
    strips, n, width,
    rhs, inverse, dis_fwd, agg_fwd, phase_fwd, gain_fwd, dis_back, agg_back, phase_back, gain_back,
    first_ref, second_ref,
    x_f, x_b, inv, agg_f, agg_b, p, z, u_b,
    t_own, t_out, t_in, m_own, m_out, m_in, n_own, n_out, n_in, l_in, t_all, m_all, n_all, l_all,
    b_own, b_out, b_in, q_own, q_out, q_in, r_in, c_in,
    c_out, c_all, d_out, d_all,
    turns, coef, load_sem, sems,
):
    s = lax.axis_index("strip")
    me = lax.axis_index("cross")
    is_first = s == 0
    is_direct = s == 1
    is_last = s == strips - 1
    is_turn = s == strips - 2
    inner = jnp.logical_and(s > 1, s < strips - 1)
    angles = rhs.shape[1]
    modes = agg_f.shape[1]
    half = modes // 2
    unk = p.shape[1]
    blocks = unk // width

    barrier = pltpu.get_barrier_semaphore()

    def greet(strip, peer):
        pl.semaphore_signal(barrier, inc=1, device_id=(strip, peer), device_id_type=MESH)

    def others(fn):
        def step(j, carry):
            fn(lax.rem(me + j, n))
            return carry
        lax.fori_loop(1, n, step, 0)

    def everyone(fn):
        def step(j, carry):
            fn(lax.rem(me + j, n))
            return carry
        lax.fori_loop(0, n, step, 0)

    load_rhs = pltpu.make_async_copy(rhs.at[0], x_f.at[pl.ds(0, angles)], load_sem.at[0])
    load_dis = pltpu.make_async_copy(
        dis_fwd.at[0, 0], x_f.at[pl.ds(angles, modes)], load_sem.at[1]
    )
    load_agg = pltpu.make_async_copy(agg_fwd.at[0], agg_f, load_sem.at[2])
    load_dis_b = pltpu.make_async_copy(dis_back.at[0, 0], x_b, load_sem.at[3])
    load_agg_b = pltpu.make_async_copy(agg_back.at[0], agg_b, load_sem.at[4])
    inv_loads = [
        pltpu.make_async_copy(
            inverse.at[0, 0, :, pl.ds(j * width, width)], inv.at[j], load_sem.at[5 + j]
        )
        for j in range(blocks)
    ]
    turn_loads = [
        pltpu.make_async_copy(ref, turns.at[j], load_sem.at[5 + blocks + j])
        for j, ref in enumerate((phase_fwd, gain_fwd, phase_back, gain_back))
    ]
    load_rhs.start()

    @pl.when(s > 0)
    def _():
        load_dis.start()

    for copy in inv_loads:
        copy.start()

    @pl.when(s > 0)
    def _():
        everyone(lambda peer: greet(s - 1, peer))

    @pl.when(s < strips - 1)
    def _():
        everyone(lambda peer: greet(s + 1, peer))

    others(lambda peer: greet(s, peer))

    @pl.when(s < strips - 1)
    def _():
        load_agg.start()

    @pl.when(s > 0)
    def _():
        load_agg_b.start()

    @pl.when(s < strips - 1)
    def _():
        load_dis_b.start()

    for copy in turn_loads:
        copy.start()

    def remote(kind, src, dst, strip, peer):
        return pltpu.make_async_remote_copy(
            src_ref=src,
            dst_ref=dst,
            send_sem=sems.at[kind, 0, peer],
            recv_sem=sems.at[kind, 1, me],
            device_id=(strip, peer),
            device_id_type=MESH,
        )

    def arrived(kind, dst, peer):
        pltpu.make_async_remote_copy(
            src_ref=dst.at[peer],
            dst_ref=dst.at[peer],
            send_sem=sems.at[kind, 0, peer],
            recv_sem=sems.at[kind, 1, peer],
            device_id=(s, peer),
            device_id_type=MESH,
        ).wait_recv()

    def scatter(kind, out, into):
        others(lambda peer: remote(kind, out.at[peer], into.at[me], s, peer).start())

    def scatter_sent(kind, out, into):
        others(lambda peer: remote(kind, out.at[peer], into.at[me], s, peer).wait_send())

    def cross_scatter(kind, out, into, strip):
        everyone(lambda peer: remote(kind, out.at[peer], into.at[me], strip, peer).start())

    def cross_scatter_sent(kind, out, into, strip):
        everyone(lambda peer: remote(kind, out.at[peer], into.at[me], strip, peer).wait_send())

    def spread(kind, src, into, strip):
        everyone(lambda peer: remote(kind, src, into.at[me], strip, peer).start())

    def spread_sent(kind, src, into, strip):
        everyone(lambda peer: remote(kind, src, into.at[me], strip, peer).wait_send())

    def total(kind, own, into):
        others(lambda peer: arrived(kind, into, peer))
        value = own[me]
        for j in range(1, n):
            value = value + into[lax.rem(me + j, n)].astype(F32)
        return value

    def cross_total(kind, into):
        everyone(lambda peer: arrived(kind, into, peer))
        value = into[0].astype(F32)
        for j in range(1, n):
            value = value + into[j].astype(F32)
        return value

    def share(kind, buf):
        others(lambda peer: remote(kind, buf.at[me], buf.at[me], s, peer).start())

    def share_sent(kind, buf):
        others(lambda peer: remote(kind, buf.at[me], buf.at[me], s, peer).wait_send())

    def shared(kind, buf):
        others(lambda peer: arrived(kind, buf, peer))

    def split(value, own, out):
        part = value.shape[0] // n
        for k in range(n):
            piece = value[k * part:(k + 1) * part]
            own[k] = piece
            out[k] = piece.astype(BF)

    def joined(buf):
        return jnp.concatenate([buf[k] for k in range(n)], axis=0)

    def rotated(value, at):
        real, imag = value[:, :half], value[:, half:]
        cosine, sine = coef[at], coef[at + 1]
        return jnp.concatenate(
            [cosine * real - sine * imag, sine * real + cosine * imag], axis=1
        )

    def columns(j):
        return slice(j * width, (j + 1) * width)

    def back_matrix():
        for j in range(blocks):
            u_b[:, columns(j)] = dot(x_b[...], inv[j]).astype(BF)

    load_rhs.wait()

    @pl.when(is_first)
    def _():
        for j in range(blocks):
            inv_loads[j].wait()
            product = dot(x_f[:angles], inv[j])
            p[:, columns(j)] = product
            z[:angles, columns(j)] = product.astype(BF)
        load_agg.wait()
        split(dot(z[:angles], agg_f[...]), b_own, b_out)

    @pl.when(s > 0)
    def _():
        load_dis.wait()
        for j in range(blocks):
            inv_loads[j].wait()
            product = dot(x_f[...], inv[j])
            p[:, columns(j)] = product[:angles]
            z[:, columns(j)] = product.astype(BF)

    greeted = (n - 1) + jnp.where(s > 0, n, 0) + jnp.where(s < strips - 1, n, 0)
    pl.semaphore_wait(barrier, greeted)

    @pl.when(is_first)
    def _():
        cross_scatter(C_IN, b_out, c_in, s + 1)
        load_dis_b.wait()
        back_matrix()
        first_ref[0] = p[...]

    @pl.when(inner)
    def _():
        load_agg.wait()
        value = dot(z[...], agg_f[...])
        split(value[angles:], t_own, t_out)
        split(value[:angles], b_own, b_out)
        scatter(T_RS, t_out, t_in)

    @pl.when(s > 1)
    def _():
        load_agg_b.wait()
        value = dot(z[...], agg_b[...])
        split(value[angles:], m_own, m_out)
        split(value[:angles], q_own, q_out)

    @pl.when(is_last)
    def _():
        cross_scatter(L_RS, m_out, l_in, s - 1)
        cross_scatter(R_RS, q_out, r_in, s - 1)

    @pl.when(inner)
    def _():
        scatter(B_RS, b_out, b_in)
        scatter(M_RS, m_out, m_in)
        scatter(Q_RS, q_out, q_in)

    for copy in turn_loads:
        copy.wait()
    for at in (0, 2):
        coef[at] = jnp.cos(turns[at]) * turns[at + 1]
        coef[at + 1] = jnp.sin(turns[at]) * turns[at + 1]

    @pl.when(inner)
    def _():
        load_dis_b.wait()
        back_matrix()
        split(dot(u_b[...], agg_b[...]), n_own, n_out)
        scatter(N_RS, n_out, n_in)
        t_all[me] = total(T_RS, t_own, t_in).astype(BF)
        share(T_AG, t_all)
        m_all[me] = total(M_RS, m_own, m_in).astype(BF)
        share(M_AG, m_all)

    @pl.when(is_turn)
    def _():
        l_all[me] = cross_total(L_RS, l_in).astype(BF)
        share(L_AG, l_all)

    @pl.when(inner)
    def _():
        n_all[me] = total(N_RS, n_own, n_in).astype(BF)
        share(N_AG, n_all)
        b_own[me] = total(B_RS, b_own, b_in)
        q_own[me] = total(Q_RS, q_own, q_in)

    @pl.when(is_direct)
    def _():
        load_dis_b.wait()
        back_matrix()
        c_all[me] = cross_total(C_IN, c_in).astype(BF)
        share(C_SH, c_all)
        load_agg_b.wait()
        split(dot(u_b[...], agg_b[...]), n_own, n_out)
        scatter(N_RS, n_out, n_in)
        load_agg.wait()
        shared(C_SH, c_all)
        first_ref[0] = p[...] - dot(joined(c_all), z[angles:])
        rounded = first_ref[0].astype(BF)
        split(dot(rounded, agg_f[...]), b_own, b_out)
        leaving = b_own[me] + rotated(c_all[me].astype(F32), 0)
        b_out[me] = leaving.astype(BF)
        cross_scatter(C_IN, b_out, c_in, s + 1)
        split(dot(rounded, agg_b[...]), q_own, q_out)
        scatter(Q_RS, q_out, q_in)
        n_all[me] = total(N_RS, n_own, n_in).astype(BF)
        share(N_AG, n_all)
        q_own[me] = total(Q_RS, q_own, q_in)
        shared(N_AG, n_all)

    @pl.when(inner)
    def _():
        shared(T_AG, t_all)
        shared(M_AG, m_all)

        @pl.when(s == 2)
        def _():
            c_all[me] = cross_total(C_IN, c_in).astype(BF)

        @pl.when(s > 2)
        def _():
            arrived(C_ON, c_all, me)

        held = c_all[me]
        leaving = rotated(held.astype(F32), 0) + b_own[me]
        c_out[...] = (leaving - dot(held, joined(t_all))).astype(BF)

        @pl.when(is_turn)
        def _():
            spread(C_ON, c_out, c_all, s + 1)

        @pl.when(s < strips - 2)
        def _():
            remote(C_ON, c_out, c_all.at[me], s + 1, me).start()

        q_own[me] = q_own[me] - dot(held, joined(m_all))

    @pl.when(is_turn)
    def _():
        turned = cross_total(R_RS, r_in)
        shared(L_AG, l_all)
        d_all[me] = (turned - dot(c_out[...], joined(l_all))).astype(BF)

    @pl.when(inner)
    def _():
        shared(N_AG, n_all)

    @pl.when(jnp.logical_and(s > 0, s < strips - 2))
    def _():
        arrived(D_ON, d_all, me)

    @pl.when(jnp.logical_and(s > 0, s < strips - 1))
    def _():
        held = d_all[me]
        leaving = rotated(held.astype(F32), 2) + q_own[me]
        d_out[...] = (leaving - dot(held, joined(n_all))).astype(BF)

        @pl.when(is_direct)
        def _():
            spread(D_ON, d_out, d_all, s - 1)

        @pl.when(s > 1)
        def _():
            remote(D_ON, d_out, d_all.at[me], s - 1, me).start()
            share(C_SH, c_all)

        share(D_SH, d_all)

    @pl.when(is_last)
    def _():
        everyone(lambda peer: arrived(C_ON, c_all, peer))

    @pl.when(inner)
    def _():
        shared(C_SH, c_all)

    @pl.when(s > 1)
    def _():
        first_ref[0] = p[...] - dot(joined(c_all), z[angles:])

    @pl.when(is_last)
    def _():
        second_ref[0] = first_ref[0]

    @pl.when(is_first)
    def _():
        everyone(lambda peer: arrived(D_ON, d_all, peer))

    @pl.when(jnp.logical_and(s > 0, s < strips - 1))
    def _():
        shared(D_SH, d_all)

    @pl.when(s < strips - 1)
    def _():
        second_ref[0] = first_ref[0] - dot(joined(d_all), u_b[...])

    @pl.when(s < 2)
    def _():
        cross_scatter_sent(C_IN, b_out, c_in, s + 1)

    @pl.when(inner)
    def _():
        scatter_sent(T_RS, t_out, t_in)
        share_sent(T_AG, t_all)
        scatter_sent(M_RS, m_out, m_in)
        share_sent(M_AG, m_all)
        scatter_sent(B_RS, b_out, b_in)

    @pl.when(jnp.logical_and(s > 0, s < strips - 1))
    def _():
        scatter_sent(N_RS, n_out, n_in)
        share_sent(N_AG, n_all)
        scatter_sent(Q_RS, q_out, q_in)
        share_sent(C_SH, c_all)
        share_sent(D_SH, d_all)

    @pl.when(is_turn)
    def _():
        share_sent(L_AG, l_all)
        spread_sent(C_ON, c_out, c_all, s + 1)

    @pl.when(jnp.logical_and(s > 1, s < strips - 2))
    def _():
        remote(C_ON, c_out, c_all.at[me], s + 1, me).wait_send()

    @pl.when(is_direct)
    def _():
        spread_sent(D_ON, d_out, d_all, s - 1)

    @pl.when(inner)
    def _():
        remote(D_ON, d_out, d_all.at[me], s - 1, me).wait_send()

    @pl.when(is_last)
    def _():
        cross_scatter_sent(L_RS, m_out, l_in, s - 1)
        cross_scatter_sent(R_RS, q_out, r_in, s - 1)


def body(strips, n, rhs, inverse, dis_fwd, agg_fwd, phase_fwd, gain_fwd, dis_back, agg_back, phase_back, gain_back):
    _, angles, unk = rhs.shape
    modes = agg_fwd.shape[2]
    width = 256 if unk % 256 == 0 else unk
    blocks = unk // width
    rows, part = angles // n, modes // n
    hbm = pl.BlockSpec(memory_space=pl.ANY)
    vmem = pl.BlockSpec(memory_space=pltpu.VMEM)
    out = pltpu.VMEM((1, angles, unk), F32)
    return pl.pallas_call(
        functools.partial(kernel, strips, n, width),
        out_shape=(out, out),
        in_specs=[hbm] * 10,
        out_specs=(vmem, vmem),
        scratch_shapes=[
            pltpu.VMEM((angles + modes, unk), BF),
            pltpu.VMEM((modes, unk), BF),
            pltpu.VMEM((blocks, unk, width), BF),
            pltpu.VMEM((unk, modes), BF),
            pltpu.VMEM((unk, modes), BF),
            pltpu.VMEM((angles, unk), F32),
            pltpu.VMEM((angles + modes, unk), BF),
            pltpu.VMEM((modes, unk), BF),
        ]
        + [pltpu.VMEM((n, part, modes), kind) for kind in (F32, BF, BF) * 3 + (BF,) * 5]
        + [pltpu.VMEM((n, rows, modes), kind) for kind in (F32, BF, BF) * 2 + (BF, BF)]
        + [pltpu.VMEM((rows, modes), BF), pltpu.VMEM((n, rows, modes), BF)] * 2
        + [pltpu.VMEM((4, 1, modes // 2), F32)] * 2
        + [pltpu.SemaphoreType.DMA((9 + blocks,)), pltpu.SemaphoreType.DMA((KINDS, 2, n))],
        compiler_params=pltpu.CompilerParams(
            collective_id=0, has_side_effects=True, vmem_limit_bytes=60 * 1024 * 1024
        ),
    )(rhs, inverse, dis_fwd, agg_fwd, phase_fwd, gain_fwd, dis_back, agg_back, phase_back, gain_back)


def solution(mesh):
    strips, n = mesh.shape["strip"], mesh.shape["cross"]
    return jax.shard_map(
        functools.partial(body, strips, n),
        mesh=mesh,
        in_specs=(
            P("strip", None, "cross"),
            P("strip", "cross", None, None),
            P("strip", "cross", None, None),
            P("strip", "cross", None),
            P("strip", None),
            P("strip", None),
            P("strip", "cross", None, None),
            P("strip", "cross", None),
            P("strip", None),
            P("strip", None),
        ),
        out_specs=(P("strip", None, "cross"), P("strip", None, "cross")),
        check_vma=False,
    )
```

time: 36.9 us -> 36.3 us (0.984)
  Pallas kernels: 34.6 us -> 34 us
    pallas_call x1, Pallas kernels: 34.6 us -> 34 us  [body(): pl.pallas_call(functools.partial(kernel, strips, n, width), out_shape=(ou...]
where the time goes in v1:
time: 36.3 us; the launch traced here: 36.1 us
  Pallas kernels  34 us (94%)
  local copies, waits for them, and re-layouts  1.54 us (4%)
  between operations  0.64 us (2%)
    pallas_call x1, Pallas kernels, body(): pl.pallas_call(functools.partial(kernel, strips, n, width), out_shape=(ou...  34 us
    unnamed x2, local copies, waits for them, and re-layouts  1.54 us

profile of v1, /device:TPU:0, one launch (start us, length us, event | category | flops | bytes accessed | tf_op | source)
XLA Modules:
  0.0 36.1 jit_solution(10564388681501222071)
XLA Ops:
  0.6 34.0 %shard_map.113 = (f32[1,64,1792]{2,1,0:T(8,128)S(1)}, f32[1,64,1792]{2,1,0:T(8,128)S(1)}) custom-call(bf16[1,64,1792]{2,1,0:T(8,128)(2,1)} %rhs.1, bf16[1,1,1792,1792]{3,2,1,0:T(8,128)(2,1)} %inverse.1, bf16[1,1,256,1792]{3,2,1,0:T(8,128)(2,1)} %dis_fwd.1, bf16[1,1792,256]{2,1,0:T(8,128)(2,1)} %agg_fwd.1, f32[1,128]{1,0:T(1,128)} %phase_fwd.1, ...), custom_call_target="tpu_custom_call" | custom-call | tf_op jit(solution)/shard_map/pallas_call | solution.py:448
  34.6 0.8 %copy.14 = f32[1,64,1792]{2,1,0:T(8,128)} copy(f32[1,64,1792]{2,1,0:T(8,128)S(1)} %get-tuple-element.2) | data formatting | bytes 917504
  35.4 0.8 %copy.15 = f32[1,64,1792]{2,1,0:T(8,128)} copy(f32[1,64,1792]{2,1,0:T(8,128)S(1)} %get-tuple-element.3) | data formatting | bytes 917504

commit v2 on v1

v2 whole, which is shorter than its diff:
```python
import functools

import jax
import jax.numpy as jnp
from jax import lax
from jax.experimental import pallas as pl
from jax.experimental.pallas import tpu as pltpu
from jax.sharding import PartitionSpec as P

MESH = pl.DeviceIdType.MESH
BF = jnp.bfloat16
F32 = jnp.float32
KINDS = 16
(
    T_RS, T_AG, M_RS, M_AG, N_RS, N_AG, L_RS, L_AG,
    B_RS, Q_RS, R_RS, C_IN, C_ON, C_SH, D_ON, D_SH,
) = range(KINDS)


def dot(a, b):
    return jnp.dot(a, b, preferred_element_type=F32)


def kernel(
    strips, n, width,
    rhs, inverse, dis_fwd, agg_fwd, phase_fwd, gain_fwd, dis_back, agg_back, phase_back, gain_back,
    first_ref, second_ref,
    x_r, x_f, x_b, inv, agg_f, agg_b, p, z, u_f, u_b,
    t_own, t_out, t_in, m_own, m_out, m_in, n_own, n_out, n_in, l_in, t_all, m_all, n_all, l_all,
    b_own, b_out, b_in, q_own, q_out, q_in, r_in, c_in,
    c_out, c_all, d_out, d_all,
    turns, coef, load_sem, sems,
):
    s = lax.axis_index("strip")
    me = lax.axis_index("cross")
    is_first = s == 0
    is_direct = s == 1
    is_last = s == strips - 1
    is_turn = s == strips - 2
    inner = jnp.logical_and(s > 1, s < strips - 1)
    angles = rhs.shape[1]
    modes = agg_f.shape[1]
    half = modes // 2
    unk = p.shape[1]
    blocks = unk // width
    leaders = n // 2
    slot = me // 2
    follows = lax.rem(me, 2)
    leads = follows == 0

    barrier = pltpu.get_barrier_semaphore()

    def greet(strip, peer):
        pl.semaphore_signal(barrier, inc=1, device_id=(strip, peer), device_id_type=MESH)

    def others(fn):
        def step(j, carry):
            fn(lax.rem(me + j, n))
            return carry
        lax.fori_loop(1, n, step, 0)

    def everyone(fn):
        def step(j, carry):
            fn(lax.rem(me + j, n))
            return carry
        lax.fori_loop(0, n, step, 0)

    load_rhs = pltpu.make_async_copy(rhs.at[0], x_r, load_sem.at[0])
    load_dis = pltpu.make_async_copy(dis_fwd.at[0, 0], x_f, load_sem.at[1])
    load_agg = pltpu.make_async_copy(agg_fwd.at[0], agg_f, load_sem.at[2])
    load_dis_b = pltpu.make_async_copy(dis_back.at[0, 0], x_b, load_sem.at[3])
    load_agg_b = pltpu.make_async_copy(agg_back.at[0], agg_b, load_sem.at[4])
    inv_loads = [
        pltpu.make_async_copy(
            inverse.at[0, 0, :, pl.ds(j * width, width)], inv.at[j], load_sem.at[5 + j]
        )
        for j in range(blocks)
    ]
    turn_loads = [
        pltpu.make_async_copy(ref, turns.at[j], load_sem.at[5 + blocks + j])
        for j, ref in enumerate((phase_fwd, gain_fwd, phase_back, gain_back))
    ]
    @pl.when(is_first)
    def _():
        load_rhs.start()

    @pl.when(s > 0)
    def _():
        load_dis.start()

    for copy in inv_loads:
        copy.start()

    @pl.when(s > 0)
    def _():
        everyone(lambda peer: greet(s - 1, peer))

    @pl.when(s < strips - 1)
    def _():
        everyone(lambda peer: greet(s + 1, peer))

    others(lambda peer: greet(s, peer))

    @pl.when(s < strips - 1)
    def _():
        load_agg.start()

    @pl.when(s > 0)
    def _():
        load_agg_b.start()
        load_rhs.start()

    @pl.when(s < strips - 1)
    def _():
        load_dis_b.start()

    for copy in turn_loads:
        copy.start()

    def remote(kind, src, dst, strip, peer):
        return pltpu.make_async_remote_copy(
            src_ref=src,
            dst_ref=dst,
            send_sem=sems.at[kind, 0, peer],
            recv_sem=sems.at[kind, 1, me],
            device_id=(strip, peer),
            device_id_type=MESH,
        )

    def other_leaders(fn):
        def step(j, carry):
            fn(2 * lax.rem(slot + j, leaders))
            return carry
        lax.fori_loop(1 - follows, leaders, step, 0)

    def every_leader(fn):
        def step(j, carry):
            fn(2 * lax.rem(slot + j, leaders))
            return carry
        lax.fori_loop(0, leaders, step, 0)

    def arrived(kind, dst, peer):
        pltpu.make_async_remote_copy(
            src_ref=dst,
            dst_ref=dst,
            send_sem=sems.at[kind, 0, peer],
            recv_sem=sems.at[kind, 1, peer],
            device_id=(s, peer),
            device_id_type=MESH,
        ).wait_recv()

    def send(copy):
        copy.start()

    def sent(copy):
        copy.wait_send()

    def scatter(kind, out, into, act=send):
        others(lambda peer: act(remote(kind, out.at[peer], into.at[me], s, peer)))

    def cross_scatter(kind, out, into, strip, act=send):
        everyone(lambda peer: act(remote(kind, out.at[peer], into.at[me], strip, peer)))

    def row_scatter(kind, out, into, act=send):
        other_leaders(
            lambda peer: act(remote(kind, out.at[peer // 2], into.at[me], s, peer))
        )

    def cross_row_scatter(kind, out, into, strip, act=send):
        every_leader(
            lambda peer: act(remote(kind, out.at[peer // 2], into.at[me], strip, peer))
        )

    def gather(kind, buf, act=send):
        other_leaders(lambda peer: act(remote(kind, buf.at[me], buf.at[me], s, peer)))

    def share(kind, buf, act=send):
        others(lambda peer: act(remote(kind, buf.at[slot], buf.at[slot], s, peer)))

    def spread(kind, src, into, strip, act=send):
        everyone(lambda peer: act(remote(kind, src, into.at[slot], strip, peer)))

    def hop(kind, src, into, strip, act=send):
        act(remote(kind, src, into.at[slot], strip, me))

    def total(kind, own, into):
        others(lambda peer: arrived(kind, into.at[peer], peer))
        value = own
        for j in range(1, n):
            value = value + into[lax.rem(me + j, n)].astype(F32)
        return value

    def cross_total(kind, into):
        everyone(lambda peer: arrived(kind, into.at[peer], peer))
        value = into[0].astype(F32)
        for j in range(1, n):
            value = value + into[j].astype(F32)
        return value

    def gathered(kind, buf):
        others(lambda peer: arrived(kind, buf.at[peer], peer))

    def shared(kind, buf):
        other_leaders(lambda peer: arrived(kind, buf.at[peer // 2], peer))

    def all_shared(kind, buf):
        every_leader(lambda peer: arrived(kind, buf.at[peer // 2], peer))

    def split(value, own, out):
        pieces = own.shape[0]
        part = value.shape[0] // pieces
        for k in range(pieces):
            piece = value[k * part:(k + 1) * part]
            own[k] = piece
            out[k] = piece.astype(BF)

    def joined(buf):
        return jnp.concatenate([buf[k] for k in range(buf.shape[0])], axis=0)

    def rotated(value, at):
        real, imag = value[:, :half], value[:, half:]
        cosine, sine = coef[at], coef[at + 1]
        return jnp.concatenate(
            [cosine * real - sine * imag, sine * real + cosine * imag], axis=1
        )

    def columns(j):
        return slice(j * width, (j + 1) * width)

    def base_field():
        for j in range(blocks):
            product = dot(x_r[...], inv[j])
            p[:, columns(j)] = product
            z[:, columns(j)] = product.astype(BF)

    def back_matrix():
        for j in range(blocks):
            u_b[:, columns(j)] = dot(x_b[...], inv[j]).astype(BF)

    @pl.when(is_first)
    def _():
        load_rhs.wait()
        inv_loads[0].wait()
        product = dot(x_r[...], inv[0])
        for j in range(blocks):
            if j + 1 < blocks:
                inv_loads[j + 1].wait()
                following = dot(x_r[...], inv[j + 1])
            p[:, columns(j)] = product
            z[:, columns(j)] = product.astype(BF)
            product = following
        load_agg.wait()
        split(dot(z[...], agg_f[...]), b_own, b_out)

    @pl.when(s > 0)
    def _():
        load_dis.wait()
        inv_loads[0].wait()
        product = dot(x_f[...], inv[0])
        for j in range(blocks):
            if j + 1 < blocks:
                inv_loads[j + 1].wait()
                following = dot(x_f[...], inv[j + 1])
            u_f[:, columns(j)] = product.astype(BF)
            product = following

    @pl.when(inner)
    def _():
        load_agg.wait()
        split(dot(u_f[...], agg_f[...]), t_own, t_out)

    @pl.when(s > 0)
    def _():
        load_agg_b.wait()

    @pl.when(is_last)
    def _():
        split(dot(u_f[...], agg_b[...]), m_own, m_out)

    greeted = (n - 1) + jnp.where(s > 0, n, 0) + jnp.where(s < strips - 1, n, 0)
    pl.semaphore_wait(barrier, greeted)

    for copy in turn_loads:
        copy.wait()

    def rotations():
        for at in (0, 2):
            coef[at] = jnp.cos(turns[at]) * turns[at + 1]
            coef[at + 1] = jnp.sin(turns[at]) * turns[at + 1]

    @pl.when(is_first)
    def _():
        cross_row_scatter(C_IN, b_out, c_in, s + 1)
        load_dis_b.wait()
        back_matrix()
        first_ref[0] = p[...]

    @pl.when(inner)
    def _():
        scatter(T_RS, t_out, t_in)
        split(dot(u_f[...], agg_b[...]), m_own, m_out)
        scatter(M_RS, m_out, m_in)
        load_dis_b.wait()
        back_matrix()
        split(dot(u_b[...], agg_b[...]), n_own, n_out)
        scatter(N_RS, n_out, n_in)
        load_rhs.wait()
        rotations()
        t_all[me] = total(T_RS, t_own[me], t_in).astype(BF)
        gather(T_AG, t_all)
        base_field()
        split(dot(z[...], agg_f[...]), b_own, b_out)
        row_scatter(B_RS, b_out, b_in)
        split(dot(z[...], agg_b[...]), q_own, q_out)
        row_scatter(Q_RS, q_out, q_in)

    @pl.when(is_turn)
    def _():
        l_all[me] = cross_total(L_RS, l_in).astype(BF)
        gather(L_AG, l_all)

    @pl.when(inner)
    def _():
        m_all[me] = total(M_RS, m_own[me], m_in).astype(BF)
        gather(M_AG, m_all)
        n_all[me] = total(N_RS, n_own[me], n_in).astype(BF)
        gather(N_AG, n_all)

    @pl.when(is_last)
    def _():
        cross_scatter(L_RS, m_out, l_in, s - 1)
        load_rhs.wait()
        base_field()
        split(dot(z[...], agg_b[...]), q_own, q_out)
        cross_row_scatter(R_RS, q_out, r_in, s - 1)

    @pl.when(is_direct)
    def _():
        load_rhs.wait()
        base_field()
        rotations()

        @pl.when(leads)
        def _():
            c_all[slot] = cross_total(C_IN, c_in).astype(BF)
            share(C_SH, c_all)

        load_dis_b.wait()
        back_matrix()
        load_agg.wait()
        shared(C_SH, c_all)
        first_ref[0] = p[...] - dot(joined(c_all), u_f[...])
        rounded = first_ref[0].astype(BF)
        split(dot(rounded, agg_f[...]), b_own, b_out)

        @pl.when(leads)
        def _():
            leaving = b_own[slot] + rotated(c_all[slot].astype(F32), 0)
            b_out[slot] = leaving.astype(BF)

        cross_row_scatter(C_IN, b_out, c_in, s + 1)
        split(dot(rounded, agg_b[...]), q_own, q_out)
        row_scatter(Q_RS, q_out, q_in)
        split(dot(u_b[...], agg_b[...]), n_own, n_out)
        scatter(N_RS, n_out, n_in)
        n_all[me] = total(N_RS, n_own[me], n_in).astype(BF)
        gather(N_AG, n_all)

        @pl.when(leads)
        def _():
            q_own[slot] = total(Q_RS, q_own[slot], q_in)
            gathered(N_AG, n_all)

    @pl.when(jnp.logical_and(inner, leads))
    def _():
        b_own[slot] = total(B_RS, b_own[slot], b_in)
        q_own[slot] = total(Q_RS, q_own[slot], q_in)
        gathered(T_AG, t_all)

        @pl.when(s == 2)
        def _():
            c_all[slot] = cross_total(C_IN, c_in).astype(BF)

        @pl.when(s > 2)
        def _():
            arrived(C_ON, c_all.at[slot], me)

        held = c_all[slot]
        leaving = rotated(held.astype(F32), 0) + b_own[slot]
        c_out[...] = (leaving - dot(held, joined(t_all))).astype(BF)

        @pl.when(s < strips - 2)
        def _():
            hop(C_ON, c_out, c_all, s + 1)

        gathered(M_AG, m_all)
        q_own[slot] = q_own[slot] - dot(held, joined(m_all))

        @pl.when(is_turn)
        def _():
            turned = cross_total(R_RS, r_in)
            gathered(L_AG, l_all)
            d_all[slot] = (turned - dot(c_out[...], joined(l_all))).astype(BF)

        gathered(N_AG, n_all)

    between = jnp.logical_and(s > 0, s < strips - 1)

    @pl.when(jnp.logical_and(between, leads))
    def _():
        @pl.when(s < strips - 2)
        def _():
            arrived(D_ON, d_all.at[slot], me)

        held = d_all[slot]
        leaving = rotated(held.astype(F32), 2) + q_own[slot]
        d_out[...] = (leaving - dot(held, joined(n_all))).astype(BF)

        @pl.when(is_direct)
        def _():
            spread(D_ON, d_out, d_all, s - 1)

        @pl.when(s > 1)
        def _():
            hop(D_ON, d_out, d_all, s - 1)

        @pl.when(is_turn)
        def _():
            spread(C_ON, c_out, c_all, s + 1)

        @pl.when(s > 1)
        def _():
            share(C_SH, c_all)

        share(D_SH, d_all)

    @pl.when(is_last)
    def _():
        all_shared(C_ON, c_all)

    @pl.when(inner)
    def _():
        shared(C_SH, c_all)

    @pl.when(s > 1)
    def _():
        first_ref[0] = p[...] - dot(joined(c_all), u_f[...])

    @pl.when(is_last)
    def _():
        second_ref[0] = first_ref[0]

    @pl.when(is_first)
    def _():
        all_shared(D_ON, d_all)

    @pl.when(between)
    def _():
        shared(D_SH, d_all)

    @pl.when(s < strips - 1)
    def _():
        second_ref[0] = first_ref[0] - dot(joined(d_all), u_b[...])

    @pl.when(s < 2)
    def _():
        cross_row_scatter(C_IN, b_out, c_in, s + 1, sent)

    @pl.when(inner)
    def _():
        scatter(T_RS, t_out, t_in, sent)
        gather(T_AG, t_all, sent)
        scatter(M_RS, m_out, m_in, sent)
        gather(M_AG, m_all, sent)
        row_scatter(B_RS, b_out, b_in, sent)

    @pl.when(between)
    def _():
        scatter(N_RS, n_out, n_in, sent)
        gather(N_AG, n_all, sent)
        row_scatter(Q_RS, q_out, q_in, sent)

    @pl.when(is_turn)
    def _():
        gather(L_AG, l_all, sent)

    @pl.when(jnp.logical_and(between, leads))
    def _():
        share(C_SH, c_all, sent)
        share(D_SH, d_all, sent)

        @pl.when(is_turn)
        def _():
            spread(C_ON, c_out, c_all, s + 1, sent)

        @pl.when(jnp.logical_and(s > 1, s < strips - 2))
        def _():
            hop(C_ON, c_out, c_all, s + 1, sent)

        @pl.when(is_direct)
        def _():
            spread(D_ON, d_out, d_all, s - 1, sent)

        @pl.when(s > 1)
        def _():
            hop(D_ON, d_out, d_all, s - 1, sent)

    @pl.when(is_last)
    def _():
        cross_scatter(L_RS, m_out, l_in, s - 1, sent)
        cross_row_scatter(R_RS, q_out, r_in, s - 1, sent)


def body(strips, n, rhs, inverse, dis_fwd, agg_fwd, phase_fwd, gain_fwd, dis_back, agg_back, phase_back, gain_back):
    _, angles, unk = rhs.shape
    modes = agg_fwd.shape[2]
    width = 256 if unk % 256 == 0 else unk
    blocks = unk // width
    leaders = n // 2
    rows, part = angles // leaders, modes // n
    hbm = pl.BlockSpec(memory_space=pl.ANY)
    vmem = pl.BlockSpec(memory_space=pltpu.VMEM)
    out = pltpu.VMEM((1, angles, unk), F32)
    return pl.pallas_call(
        functools.partial(kernel, strips, n, width),
        out_shape=(out, out),
        in_specs=[hbm] * 10,
        out_specs=(vmem, vmem),
        scratch_shapes=[
            pltpu.VMEM((angles, unk), BF),
            pltpu.VMEM((modes, unk), BF),
            pltpu.VMEM((modes, unk), BF),
            pltpu.VMEM((blocks, unk, width), BF),
            pltpu.VMEM((unk, modes), BF),
            pltpu.VMEM((unk, modes), BF),
            pltpu.VMEM((angles, unk), F32),
            pltpu.VMEM((angles, unk), BF),
            pltpu.VMEM((modes, unk), BF),
            pltpu.VMEM((modes, unk), BF),
        ]
        + [pltpu.VMEM((n, part, modes), kind) for kind in (F32, BF, BF) * 3 + (BF,) * 5]
        + [
            pltpu.VMEM((count, rows, modes), kind)
            for count, kind in ((leaders, F32), (leaders, BF), (n, BF)) * 2 + ((n, BF),) * 2
        ]
        + [pltpu.VMEM((rows, modes), BF), pltpu.VMEM((leaders, rows, modes), BF)] * 2
        + [pltpu.VMEM((4, 1, modes // 2), F32)] * 2
        + [pltpu.SemaphoreType.DMA((9 + blocks,)), pltpu.SemaphoreType.DMA((KINDS, 2, n))],
        compiler_params=pltpu.CompilerParams(
            collective_id=0, has_side_effects=True, vmem_limit_bytes=60 * 1024 * 1024
        ),
    )(rhs, inverse, dis_fwd, agg_fwd, phase_fwd, gain_fwd, dis_back, agg_back, phase_back, gain_back)


def solution(mesh):
    strips, n = mesh.shape["strip"], mesh.shape["cross"]
    return jax.shard_map(
        functools.partial(body, strips, n),
        mesh=mesh,
        in_specs=(
            P("strip", None, "cross"),
            P("strip", "cross", None, None),
            P("strip", "cross", None, None),
            P("strip", "cross", None),
            P("strip", None),
            P("strip", None),
            P("strip", "cross", None, None),
            P("strip", "cross", None),
            P("strip", None),
            P("strip", None),
        ),
        out_specs=(P("strip", None, "cross"), P("strip", None, "cross")),
        check_vma=False,
    )
```

time: 36.3 us -> 33.1 us (0.912)
  Pallas kernels: 34 us -> 30.8 us
    pallas_call x1, Pallas kernels: 34 us -> 30.8 us  [body(): pl.pallas_call(functools.partial(kernel, strips, n, width), out_shape=(ou...]
where the time goes in v2:
time: 33.1 us; the launch traced here: 32.9 us
  Pallas kernels  30.8 us (93%)
  local copies, waits for them, and re-layouts  1.54 us (5%)
  between operations  0.64 us (2%)
    pallas_call x1, Pallas kernels, body(): pl.pallas_call(functools.partial(kernel, strips, n, width), out_shape=(ou...  30.8 us
    unnamed x2, local copies, waits for them, and re-layouts  1.54 us

profile of v2, /device:TPU:0, one launch (start us, length us, event | category | flops | bytes accessed | tf_op | source)
XLA Modules:
  0.0 32.9 jit_solution(12625145720999691179)
XLA Ops:
  0.6 30.8 %shard_map.113 = (f32[1,64,1792]{2,1,0:T(8,128)S(1)}, f32[1,64,1792]{2,1,0:T(8,128)S(1)}) custom-call(bf16[1,64,1792]{2,1,0:T(8,128)(2,1)} %rhs.1, bf16[1,1,1792,1792]{3,2,1,0:T(8,128)(2,1)} %inverse.1, bf16[1,1,256,1792]{3,2,1,0:T(8,128)(2,1)} %dis_fwd.1, bf16[1,1792,256]{2,1,0:T(8,128)(2,1)} %agg_fwd.1, f32[1,128]{1,0:T(1,128)} %phase_fwd.1, ...), custom_call_target="tpu_custom_call" | custom-call | tf_op jit(solution)/shard_map/pallas_call | solution.py:524
  31.4 0.8 %copy.14 = f32[1,64,1792]{2,1,0:T(8,128)} copy(f32[1,64,1792]{2,1,0:T(8,128)S(1)} %get-tuple-element.2) | data formatting | bytes 917504
  32.2 0.8 %copy.15 = f32[1,64,1792]{2,1,0:T(8,128)} copy(f32[1,64,1792]{2,1,0:T(8,128)S(1)} %get-tuple-element.3) | data formatting | bytes 917504

commit v3 on v2

--- a/solution.py
+++ b/solution.py
@@ -121,8 +121,8 @@
         return pltpu.make_async_remote_copy(
             src_ref=src,
             dst_ref=dst,
-            send_sem=sems.at[kind, 0, peer],
-            recv_sem=sems.at[kind, 1, me],
+            send_sem=sems.at[kind, 0],
+            recv_sem=sems.at[kind, 1],
             device_id=(strip, peer),
             device_id_type=MESH,
         )
@@ -139,72 +139,78 @@
             return carry
         lax.fori_loop(0, leaders, step, 0)
 
-    def arrived(kind, dst, peer):
-        pltpu.make_async_remote_copy(
-            src_ref=dst,
-            dst_ref=dst,
-            send_sem=sems.at[kind, 0, peer],
-            recv_sem=sems.at[kind, 1, peer],
-            device_id=(s, peer),
+    def waiting(kind, ref):
+        return pltpu.make_async_remote_copy(
+            src_ref=ref,
+            dst_ref=ref,
+            send_sem=sems.at[kind, 0],
+            recv_sem=sems.at[kind, 1],
+            device_id=(s, lax.rem(me + 1, n)),
             device_id_type=MESH,
-        ).wait_recv()
-
-    def send(copy):
-        copy.start()
-
-    def sent(copy):
-        copy.wait_send()
-
-    def scatter(kind, out, into, act=send):
-        others(lambda peer: act(remote(kind, out.at[peer], into.at[me], s, peer)))
-
-    def cross_scatter(kind, out, into, strip, act=send):
-        everyone(lambda peer: act(remote(kind, out.at[peer], into.at[me], strip, peer)))
-
-    def row_scatter(kind, out, into, act=send):
+        )
+
+    def arrived(kind, ref):
+        waiting(kind, ref).wait_recv()
+
+    def sent(kind, ref):
+        waiting(kind, ref).wait_send()
+
+    def by_role(act, kind, buf):
+        @pl.when(leads)
+        def _():
+            act(kind, buf.at[pl.ds(0, leaders - 1)])
+
+        @pl.when(follows == 1)
+        def _():
+            act(kind, buf.at[pl.ds(0, leaders)])
+
+    def scatter(kind, out, into):
+        others(lambda peer: remote(kind, out.at[peer], into.at[me], s, peer).start())
+
+    def cross_scatter(kind, out, into, strip):
+        everyone(lambda peer: remote(kind, out.at[peer], into.at[me], strip, peer).start())
+
+    def row_scatter(kind, out, into):
         other_leaders(
-            lambda peer: act(remote(kind, out.at[peer // 2], into.at[me], s, peer))
+            lambda peer: remote(kind, out.at[peer // 2], into.at[me], s, peer).start()
         )
 
-    def cross_row_scatter(kind, out, into, strip, act=send):
+    def cross_row_scatter(kind, out, into, strip):
         every_leader(
-            lambda peer: act(remote(kind, out.at[peer // 2], into.at[me], strip, peer))
+            lambda peer: remote(kind, out.at[peer // 2], into.at[me], strip, peer).start()
         )
 
-    def gather(kind, buf, act=send):
-        other_leaders(lambda peer: act(remote(kind, buf.at[me], buf.at[me], s, peer)))
-
-    def share(kind, buf, act=send):
-        others(lambda peer: act(remote(kind, buf.at[slot], buf.at[slot], s, peer)))
-
-    def spread(kind, src, into, strip, act=send):
-        everyone(lambda peer: act(remote(kind, src, into.at[slot], strip, peer)))
-
-    def hop(kind, src, into, strip, act=send):
-        act(remote(kind, src, into.at[slot], strip, me))
+    def gather(kind, buf):
+        other_leaders(lambda peer: remote(kind, buf.at[me], buf.at[me], s, peer).start())
+
+    def share(kind, buf):
+        others(lambda peer: remote(kind, buf.at[slot], buf.at[slot], s, peer).start())
+
+    def spread(kind, src, into, strip):
+        everyone(lambda peer: remote(kind, src, into.at[slot], strip, peer).start())
+
+    def hop(kind, src, into, strip):
+        remote(kind, src, into.at[slot], strip, me).start()
 
     def total(kind, own, into):
-        others(lambda peer: arrived(kind, into.at[peer], peer))
+        arrived(kind, into.at[pl.ds(0, n - 1)])
         value = own
         for j in range(1, n):
             value = value + into[lax.rem(me + j, n)].astype(F32)
         return value
 
     def cross_total(kind, into):
-        everyone(lambda peer: arrived(kind, into.at[peer], peer))
+        arrived(kind, into)
         value = into[0].astype(F32)
         for j in range(1, n):
             value = value + into[j].astype(F32)
         return value
 
     def gathered(kind, buf):
-        others(lambda peer: arrived(kind, buf.at[peer], peer))
+        arrived(kind, buf.at[pl.ds(0, n - 1)])
 
     def shared(kind, buf):
-        other_leaders(lambda peer: arrived(kind, buf.at[peer // 2], peer))
-
-    def all_shared(kind, buf):
-        every_leader(lambda peer: arrived(kind, buf.at[peer // 2], peer))
+        by_role(arrived, kind, buf)
 
     def split(value, own, out):
         pieces = own.shape[0]
@@ -227,42 +233,37 @@
     def columns(j):
         return slice(j * width, (j + 1) * width)
 
-    def base_field():
-        for j in range(blocks):
+    cuts = sorted({0, min(2, blocks), min(4, blocks), blocks})
+    groups = [range(a, b) for a, b in zip(cuts, cuts[1:])]
+
+    def base_field(group):
+        for j in group:
             product = dot(x_r[...], inv[j])
             p[:, columns(j)] = product
             z[:, columns(j)] = product.astype(BF)
 
-    def back_matrix():
-        for j in range(blocks):
+    def back_matrix(group):
+        for j in group:
             u_b[:, columns(j)] = dot(x_b[...], inv[j]).astype(BF)
 
     @pl.when(is_first)
     def _():
         load_rhs.wait()
-        inv_loads[0].wait()
-        product = dot(x_r[...], inv[0])
-        for j in range(blocks):
-            if j + 1 < blocks:
-                inv_loads[j + 1].wait()
-                following = dot(x_r[...], inv[j + 1])
-            p[:, columns(j)] = product
-            z[:, columns(j)] = product.astype(BF)
-            product = following
+        for group in groups:
+            for j in group:
+                inv_loads[j].wait()
+            base_field(group)
         load_agg.wait()
         split(dot(z[...], agg_f[...]), b_own, b_out)
 
     @pl.when(s > 0)
     def _():
         load_dis.wait()
-        inv_loads[0].wait()
-        product = dot(x_f[...], inv[0])
-        for j in range(blocks):
-            if j + 1 < blocks:
-                inv_loads[j + 1].wait()
-                following = dot(x_f[...], inv[j + 1])
-            u_f[:, columns(j)] = product.astype(BF)
-            product = following
+        for group in groups:
+            for j in group:
+                inv_loads[j].wait()
+            for j in group:
+                u_f[:, columns(j)] = dot(x_f[...], inv[j]).astype(BF)
 
     @pl.when(inner)
     def _():
@@ -292,7 +293,7 @@
     def _():
         cross_row_scatter(C_IN, b_out, c_in, s + 1)
         load_dis_b.wait()
-        back_matrix()
+        back_matrix(range(blocks))
         first_ref[0] = p[...]
 
     @pl.when(inner)
@@ -301,28 +302,29 @@
         split(dot(u_f[...], agg_b[...]), m_own, m_out)
         scatter(M_RS, m_out, m_in)
         load_dis_b.wait()
-        back_matrix()
+        back_matrix(range(blocks))
         split(dot(u_b[...], agg_b[...]), n_own, n_out)
         scatter(N_RS, n_out, n_in)
         load_rhs.wait()
         rotations()
         t_all[me] = total(T_RS, t_own[me], t_in).astype(BF)
         gather(T_AG, t_all)
-        base_field()
+        base_field(range(0, blocks // 2))
+        m_all[me] = total(M_RS, m_own[me], m_in).astype(BF)
+        gather(M_AG, m_all)
+
+    @pl.when(is_turn)
+    def _():
+        l_all[me] = cross_total(L_RS, l_in).astype(BF)
+        gather(L_AG, l_all)
+
+    @pl.when(inner)
+    def _():
+        base_field(range(blocks // 2, blocks))
         split(dot(z[...], agg_f[...]), b_own, b_out)
         row_scatter(B_RS, b_out, b_in)
         split(dot(z[...], agg_b[...]), q_own, q_out)
         row_scatter(Q_RS, q_out, q_in)
-
-    @pl.when(is_turn)
-    def _():
-        l_all[me] = cross_total(L_RS, l_in).astype(BF)
-        gather(L_AG, l_all)
-
-    @pl.when(inner)
-    def _():
-        m_all[me] = total(M_RS, m_own[me], m_in).astype(BF)
-        gather(M_AG, m_all)
         n_all[me] = total(N_RS, n_own[me], n_in).astype(BF)
         gather(N_AG, n_all)
 
@@ -330,14 +332,14 @@
     def _():
         cross_scatter(L_RS, m_out, l_in, s - 1)
         load_rhs.wait()
-        base_field()
+        base_field(range(blocks))
         split(dot(z[...], agg_b[...]), q_own, q_out)
         cross_row_scatter(R_RS, q_out, r_in, s - 1)
 
     @pl.when(is_direct)
     def _():
         load_rhs.wait()
-        base_field()
+        base_field(range(blocks))
         rotations()
 
         @pl.when(leads)
@@ -346,7 +348,7 @@
             share(C_SH, c_all)
 
         load_dis_b.wait()
-        back_matrix()
+        back_matrix(range(blocks))
         load_agg.wait()
         shared(C_SH, c_all)
         first_ref[0] = p[...] - dot(joined(c_all), u_f[...])
@@ -383,7 +385,7 @@
 
         @pl.when(s > 2)
         def _():
-            arrived(C_ON, c_all.at[slot], me)
+            arrived(C_ON, c_all.at[slot])
 
         held = c_all[slot]
         leaving = rotated(held.astype(F32), 0) + b_own[slot]
@@ -410,7 +412,7 @@
     def _():
         @pl.when(s < strips - 2)
         def _():
-            arrived(D_ON, d_all.at[slot], me)
+            arrived(D_ON, d_all.at[slot])
 
         held = d_all[slot]
         leaving = rotated(held.astype(F32), 2) + q_own[slot]
@@ -423,6 +425,7 @@
         @pl.when(s > 1)
         def _():
             hop(D_ON, d_out, d_all, s - 1)
+            sent(D_ON, d_out)
 
         @pl.when(is_turn)
         def _():
@@ -436,7 +439,7 @@
 
     @pl.when(is_last)
     def _():
-        all_shared(C_ON, c_all)
+        arrived(C_ON, c_all)
 
     @pl.when(inner)
     def _():
@@ -452,7 +455,7 @@
 
     @pl.when(is_first)
     def _():
-        all_shared(D_ON, d_all)
+        arrived(D_ON, d_all)
 
     @pl.when(between)
     def _():
@@ -464,51 +467,47 @@
 
     @pl.when(s < 2)
     def _():
-        cross_row_scatter(C_IN, b_out, c_in, s + 1, sent)
+        sent(C_IN, b_out)
 
     @pl.when(inner)
     def _():
-        scatter(T_RS, t_out, t_in, sent)
-        gather(T_AG, t_all, sent)
-        scatter(M_RS, m_out, m_in, sent)
-        gather(M_AG, m_all, sent)
-        row_scatter(B_RS, b_out, b_in, sent)
+        sent(T_RS, t_out.at[pl.ds(0, n - 1)])
+        sent(M_RS, m_out.at[pl.ds(0, n - 1)])
+        by_role(sent, T_AG, t_all)
+        by_role(sent, M_AG, m_all)
+        by_role(sent, B_RS, b_out)
 
     @pl.when(between)
     def _():
-        scatter(N_RS, n_out, n_in, sent)
-        gather(N_AG, n_all, sent)
-        row_scatter(Q_RS, q_out, q_in, sent)
+        sent(N_RS, n_out.at[pl.ds(0, n - 1)])
+        by_role(sent, N_AG, n_all)
+        by_role(sent, Q_RS, q_out)
 
     @pl.when(is_turn)
     def _():
-        gather(L_AG, l_all, sent)
+        by_role(sent, L_AG, l_all)
 
     @pl.when(jnp.logical_and(between, leads))
     def _():
-        share(C_SH, c_all, sent)
-        share(D_SH, d_all, sent)
+        sent(C_SH, c_in.at[pl.ds(0, n - 1)])
+        sent(D_SH, c_in.at[pl.ds(0, n - 1)])
 
         @pl.when(is_turn)
         def _():
-            spread(C_ON, c_out, c_all, s + 1, sent)
+            sent(C_ON, c_in)
 
         @pl.when(jnp.logical_and(s > 1, s < strips - 2))
         def _():
-            hop(C_ON, c_out, c_all, s + 1, sent)
+            sent(C_ON, c_out)
 
         @pl.when(is_direct)
         def _():
-            spread(D_ON, d_out, d_all, s - 1, sent)
-
-        @pl.when(s > 1)
-        def _():
-            hop(D_ON, d_out, d_all, s - 1, sent)
+            sent(D_ON, c_in)
 
     @pl.when(is_last)
     def _():
-        cross_scatter(L_RS, m_out, l_in, s - 1, sent)
-        cross_row_scatter(R_RS, q_out, r_in, s - 1, sent)
+        sent(L_RS, m_out)
+        sent(R_RS, q_out)
 
 
 def body(strips, n, rhs, inverse, dis_fwd, agg_fwd, phase_fwd, gain_fwd, dis_back, agg_back, phase_back, gain_back):
@@ -545,7 +544,7 @@
         ]
         + [pltpu.VMEM((rows, modes), BF), pltpu.VMEM((leaders, rows, modes), BF)] * 2
         + [pltpu.VMEM((4, 1, modes // 2), F32)] * 2
-        + [pltpu.SemaphoreType.DMA((9 + blocks,)), pltpu.SemaphoreType.DMA((KINDS, 2, n))],
+        + [pltpu.SemaphoreType.DMA((9 + blocks,)), pltpu.SemaphoreType.DMA((KINDS, 2))],
         compiler_params=pltpu.CompilerParams(
             collective_id=0, has_side_effects=True, vmem_limit_bytes=60 * 1024 * 1024
         ),

time: 33.1 us -> 30.4 us (0.918)
  Pallas kernels: 30.8 us -> 28 us
    pallas_call x1, Pallas kernels: 30.8 us -> 28 us  [body(): pl.pallas_call(functools.partial(kernel, strips, n, width), out_shape=(ou...]
where the time goes in v3:
time: 30.4 us; the launch traced here: 30.2 us
  Pallas kernels  28 us (92%)
  local copies, waits for them, and re-layouts  1.54 us (5%)
  between operations  0.64 us (2%)
    pallas_call x1, Pallas kernels, body(): pl.pallas_call(functools.partial(kernel, strips, n, width), out_shape=(ou...  28 us
    unnamed x2, local copies, waits for them, and re-layouts  1.54 us

profile of v3, /device:TPU:0, one launch (start us, length us, event | category | flops | bytes accessed | tf_op | source)
XLA Modules:
  0.0 30.2 jit_solution(2319299338086605744)
XLA Ops:
  0.6 28.0 %shard_map.113 = (f32[1,64,1792]{2,1,0:T(8,128)S(1)}, f32[1,64,1792]{2,1,0:T(8,128)S(1)}) custom-call(bf16[1,64,1792]{2,1,0:T(8,128)(2,1)} %rhs.1, bf16[1,1,1792,1792]{3,2,1,0:T(8,128)(2,1)} %inverse.1, bf16[1,1,256,1792]{3,2,1,0:T(8,128)(2,1)} %dis_fwd.1, bf16[1,1792,256]{2,1,0:T(8,128)(2,1)} %agg_fwd.1, f32[1,128]{1,0:T(1,128)} %phase_fwd.1, ...), custom_call_target="tpu_custom_call" | custom-call | tf_op jit(solution)/shard_map/pallas_call | solution.py:523
  28.7 0.8 %copy.14 = f32[1,64,1792]{2,1,0:T(8,128)} copy(f32[1,64,1792]{2,1,0:T(8,128)S(1)} %get-tuple-element.2) | data formatting | bytes 917504
  29.5 0.8 %copy.15 = f32[1,64,1792]{2,1,0:T(8,128)} copy(f32[1,64,1792]{2,1,0:T(8,128)S(1)} %get-tuple-element.3) | data formatting | bytes 917504

commit v4 on v3

--- a/solution.py
+++ b/solution.py
@@ -24,8 +24,8 @@
 def kernel(
     strips, n, width,
     rhs, inverse, dis_fwd, agg_fwd, phase_fwd, gain_fwd, dis_back, agg_back, phase_back, gain_back,
-    first_ref, second_ref,
-    x_r, x_f, x_b, inv, agg_f, agg_b, p, z, u_f, u_b,
+    p, cu, du,
+    x_r, x_f, x_b, inv, agg_f, agg_b, z, u_f, u_b,
     t_own, t_out, t_in, m_own, m_out, m_in, n_own, n_out, n_in, l_in, t_all, m_all, n_all, l_all,
     b_own, b_out, b_in, q_own, q_out, q_in, r_in, c_in,
     c_out, c_all, d_out, d_all,
@@ -294,7 +294,7 @@
         cross_row_scatter(C_IN, b_out, c_in, s + 1)
         load_dis_b.wait()
         back_matrix(range(blocks))
-        first_ref[0] = p[...]
+        cu[...] = jnp.zeros_like(cu)
 
     @pl.when(inner)
     def _():
@@ -306,25 +306,24 @@
         split(dot(u_b[...], agg_b[...]), n_own, n_out)
         scatter(N_RS, n_out, n_in)
         load_rhs.wait()
+        base_field(range(blocks))
         rotations()
         t_all[me] = total(T_RS, t_own[me], t_in).astype(BF)
         gather(T_AG, t_all)
-        base_field(range(0, blocks // 2))
-        m_all[me] = total(M_RS, m_own[me], m_in).astype(BF)
-        gather(M_AG, m_all)
-
-    @pl.when(is_turn)
-    def _():
-        l_all[me] = cross_total(L_RS, l_in).astype(BF)
-        gather(L_AG, l_all)
-
-    @pl.when(inner)
-    def _():
-        base_field(range(blocks // 2, blocks))
         split(dot(z[...], agg_f[...]), b_own, b_out)
         row_scatter(B_RS, b_out, b_in)
         split(dot(z[...], agg_b[...]), q_own, q_out)
         row_scatter(Q_RS, q_out, q_in)
+        m_all[me] = total(M_RS, m_own[me], m_in).astype(BF)
+        gather(M_AG, m_all)
+
+    @pl.when(is_turn)
+    def _():
+        l_all[me] = cross_total(L_RS, l_in).astype(BF)
+        gather(L_AG, l_all)
+
+    @pl.when(inner)
+    def _():
         n_all[me] = total(N_RS, n_own[me], n_in).astype(BF)
         gather(N_AG, n_all)
 
@@ -335,6 +334,7 @@
         base_field(range(blocks))
         split(dot(z[...], agg_b[...]), q_own, q_out)
         cross_row_scatter(R_RS, q_out, r_in, s - 1)
+        du[...] = jnp.zeros_like(du)
 
     @pl.when(is_direct)
     def _():
@@ -351,8 +351,8 @@
         back_matrix(range(blocks))
         load_agg.wait()
         shared(C_SH, c_all)
-        first_ref[0] = p[...] - dot(joined(c_all), u_f[...])
-        rounded = first_ref[0].astype(BF)
+        cu[...] = dot(joined(c_all), u_f[...])
+        rounded = (p[...] - cu[...]).astype(BF)
         split(dot(rounded, agg_f[...]), b_own, b_out)
 
         @pl.when(leads)
@@ -447,11 +447,7 @@
 
     @pl.when(s > 1)
     def _():
-        first_ref[0] = p[...] - dot(joined(c_all), u_f[...])
-
-    @pl.when(is_last)
-    def _():
-        second_ref[0] = first_ref[0]
+        cu[...] = dot(joined(c_all), u_f[...])
 
     @pl.when(is_first)
     def _():
@@ -463,7 +459,7 @@
 
     @pl.when(s < strips - 1)
     def _():
-        second_ref[0] = first_ref[0] - dot(joined(d_all), u_b[...])
+        du[...] = dot(joined(d_all), u_b[...])
 
     @pl.when(s < 2)
     def _():
@@ -519,12 +515,12 @@
     rows, part = angles // leaders, modes // n
     hbm = pl.BlockSpec(memory_space=pl.ANY)
     vmem = pl.BlockSpec(memory_space=pltpu.VMEM)
-    out = pltpu.VMEM((1, angles, unk), F32)
-    return pl.pallas_call(
+    out = pltpu.VMEM((angles, unk), F32)
+    base, cu, du = pl.pallas_call(
         functools.partial(kernel, strips, n, width),
-        out_shape=(out, out),
+        out_shape=(out,) * 3,
         in_specs=[hbm] * 10,
-        out_specs=(vmem, vmem),
+        out_specs=(vmem,) * 3,
         scratch_shapes=[
             pltpu.VMEM((angles, unk), BF),
             pltpu.VMEM((modes, unk), BF),
@@ -532,7 +528,6 @@
             pltpu.VMEM((blocks, unk, width), BF),
             pltpu.VMEM((unk, modes), BF),
             pltpu.VMEM((unk, modes), BF),
-            pltpu.VMEM((angles, unk), F32),
             pltpu.VMEM((angles, unk), BF),
             pltpu.VMEM((modes, unk), BF),
             pltpu.VMEM((modes, unk), BF),
@@ -549,6 +544,8 @@
             collective_id=0, has_side_effects=True, vmem_limit_bytes=60 * 1024 * 1024
         ),
     )(rhs, inverse, dis_fwd, agg_fwd, phase_fwd, gain_fwd, dis_back, agg_back, phase_back, gain_back)
+    first = base - cu
+    return first[None], (first - du)[None]
 
 
 def solution(mesh):

time: 30.4 us -> 29.3 us (0.964)
  local copies, waits for them, and re-layouts: 1.54 us -> 0 us
  other arithmetic: 0 us -> 1 us
  Pallas kernels: 28 us -> 27.5 us
    unnamed x2 -> x0, local copies, waits for them, and re-layouts: 1.54 us -> none
    broadcast_in_dim x0 -> x1, other arithmetic: none -> 1 us  [body(): return (first[None], (first - du)[None])]
    pallas_call x1, Pallas kernels: 28 us -> 27.5 us  [body(): pl.pallas_call(functools.partial(kernel, strips, n, width), out_shape=(ou...]
where the time goes in v4:
time: 29.3 us; the launch traced here: 29.1 us
  Pallas kernels  27.5 us (94%)
  other arithmetic  1 us (3%)
  between operations  0.64 us (2%)
    pallas_call x1, Pallas kernels, body(): pl.pallas_call(functools.partial(kernel, strips, n, width), out_shape=(ou...  27.5 us
    broadcast_in_dim x1, other arithmetic, body(): return (first[None], (first - du)[None])  1 us

profile of v4, /device:TPU:0, one launch (start us, length us, event | category | flops | bytes accessed | tf_op | source)
XLA Modules:
  0.0 29.1 jit_solution(9872822537841625105)
XLA Ops:
  0.6 27.5 %shard_map.113 = (f32[64,1792]{1,0:T(8,128)S(1)}, f32[64,1792]{1,0:T(8,128)S(1)}, f32[64,1792]{1,0:T(8,128)S(1)}) custom-call(bf16[1,64,1792]{2,1,0:T(8,128)(2,1)} %rhs.1, bf16[1,1,1792,1792]{3,2,1,0:T(8,128)(2,1)} %inverse.1, bf16[1,1,256,1792]{3,2,1,0:T(8,128)(2,1)} %dis_fwd.1, bf16[1,1792,256]{2,1,0:T(8,128)(2,1)} %agg_fwd.1, f32[1,128]{1,0:T(1,128)} %phase_fwd.1, ...), custom_call_target="tpu_custom_call" | custom-call | tf_op jit(solution)/shard_map/pallas_call | solution.py:519
  28.1 1.0 %subtract_bitcast_fusion = (f32[1,64,1792]{2,1,0:T(8,128)}, f32[1,64,1792]{2,1,0:T(8,128)}) fusion(f32[64,1792]{1,0:T(8,128)S(1)} %get-tuple-element.7, f32[64,1792]{1,0:T(8,128)S(1)} %get-tuple-element.5, f32[64,1792]{1,0:T(8,128)S(1)} %get-tuple-element.6), kind=kLoop, calls=%fused_computation | loop fusion | flops 229376 | bytes 2293760 | tf_op jit(solution)/shard_map/broadcast_in_dim | solution.py:548

commit v5 on v4

--- a/solution.py
+++ b/solution.py
@@ -10,9 +10,9 @@
 MESH = pl.DeviceIdType.MESH
 BF = jnp.bfloat16
 F32 = jnp.float32
-KINDS = 16
+KINDS = 18
 (
-    T_RS, T_AG, M_RS, M_AG, N_RS, N_AG, L_RS, L_AG,
+    T_PR, M_PR, N_PR, T_RS, T_AG, M_RS, M_AG, N_RS, N_AG, L_AG,
     B_RS, Q_RS, R_RS, C_IN, C_ON, C_SH, D_ON, D_SH,
 ) = range(KINDS)
 
@@ -26,7 +26,8 @@
     rhs, inverse, dis_fwd, agg_fwd, phase_fwd, gain_fwd, dis_back, agg_back, phase_back, gain_back,
     p, cu, du,
     x_r, x_f, x_b, inv, agg_f, agg_b, z, u_f, u_b,
-    t_own, t_out, t_in, m_own, m_out, m_in, n_own, n_out, n_in, l_in, t_all, m_all, n_all, l_all,
+    t_own, m_own, n_own, t_out, m_out, n_out, t_pair, m_pair, n_pair, t_in, m_in, n_in,
+    t_all, m_all, n_all, l_all,
     b_own, b_out, b_in, q_own, q_out, q_in, r_in, c_in,
     c_out, c_all, d_out, d_all,
     turns, coef, load_sem, sems,
@@ -164,11 +165,39 @@
         def _():
             act(kind, buf.at[pl.ds(0, leaders)])
 
-    def scatter(kind, out, into):
-        others(lambda peer: remote(kind, out.at[peer], into.at[me], s, peer).start())
-
-    def cross_scatter(kind, out, into, strip):
-        everyone(lambda peer: remote(kind, out.at[peer], into.at[me], strip, peer).start())
+    def split_pairs(value, own, out):
+        part = value.shape[0] // n
+        for k in range(n):
+            piece = value[k * part:(k + 1) * part]
+            own[k % 2, k // 2] = piece
+            out[k % 2, k // 2] = piece.astype(BF)
+
+    def pair_send(kind, out, pair):
+        remote(kind, out.at[1 - follows], pair, s, me + 1 - 2 * follows).start()
+
+    def pair_scatter(pair_kind, kind, own, out, pair, into):
+        arrived(pair_kind, pair)
+        value = own[follows] + pair[...].astype(F32)
+        own[follows] = value
+        out[follows] = value.astype(BF)
+
+        def step(j, carry):
+            at = lax.rem(slot + j, leaders)
+            remote(kind, out.at[follows, at], into.at[slot], s, 2 * at + follows).start()
+            return carry
+
+        lax.fori_loop(1, leaders, step, 0)
+
+    def pair_total(kind, own, into):
+        arrived(kind, into.at[pl.ds(0, leaders - 1)])
+        value = own[follows, slot]
+        for j in range(1, leaders):
+            value = value + into[lax.rem(slot + j, leaders)].astype(F32)
+        return value
+
+    def pair_sent(pair_kind, kind, pair):
+        sent(pair_kind, pair)
+        sent(kind, pair.at[pl.ds(0, leaders - 1)])
 
     def row_scatter(kind, out, into):
         other_leaders(
@@ -268,7 +297,7 @@
     @pl.when(inner)
     def _():
         load_agg.wait()
-        split(dot(u_f[...], agg_f[...]), t_own, t_out)
+        split_pairs(dot(u_f[...], agg_f[...]), t_own, t_out)
 
     @pl.when(s > 0)
     def _():
@@ -276,7 +305,7 @@
 
     @pl.when(is_last)
     def _():
-        split(dot(u_f[...], agg_b[...]), m_own, m_out)
+        split_pairs(dot(u_f[...], agg_b[...]), m_own, m_out)
 
     greeted = (n - 1) + jnp.where(s > 0, n, 0) + jnp.where(s < strips - 1, n, 0)
     pl.semaphore_wait(barrier, greeted)
@@ -298,43 +327,46 @@
 
     @pl.when(inner)
     def _():
-        scatter(T_RS, t_out, t_in)
-        split(dot(u_f[...], agg_b[...]), m_own, m_out)
-        scatter(M_RS, m_out, m_in)
+        pair_send(T_PR, t_out, t_pair)
+        split_pairs(dot(u_f[...], agg_b[...]), m_own, m_out)
+        pair_send(M_PR, m_out, m_pair)
         load_dis_b.wait()
-        back_matrix(range(blocks))
-        split(dot(u_b[...], agg_b[...]), n_own, n_out)
-        scatter(N_RS, n_out, n_in)
+        back_matrix(range(0, blocks // 2))
+        pair_scatter(T_PR, T_RS, t_own, t_out, t_pair, t_in)
+        pair_scatter(M_PR, M_RS, m_own, m_out, m_pair, m_in)
+        back_matrix(range(blocks // 2, blocks))
+        split_pairs(dot(u_b[...], agg_b[...]), n_own, n_out)
+        pair_send(N_PR, n_out, n_pair)
         load_rhs.wait()
-        base_field(range(blocks))
+        base_field(range(0, (blocks + 1) // 2))
+        pair_scatter(N_PR, N_RS, n_own, n_out, n_pair, n_in)
+        base_field(range((blocks + 1) // 2, blocks))
         rotations()
-        t_all[me] = total(T_RS, t_own[me], t_in).astype(BF)
+        t_all[me] = pair_total(T_RS, t_own, t_in).astype(BF)
         gather(T_AG, t_all)
         split(dot(z[...], agg_f[...]), b_own, b_out)
         row_scatter(B_RS, b_out, b_in)
         split(dot(z[...], agg_b[...]), q_own, q_out)
         row_scatter(Q_RS, q_out, q_in)
-        m_all[me] = total(M_RS, m_own[me], m_in).astype(BF)
+        m_all[me] = pair_total(M_RS, m_own, m_in).astype(BF)
         gather(M_AG, m_all)
-
-    @pl.when(is_turn)
-    def _():
-        l_all[me] = cross_total(L_RS, l_in).astype(BF)
-        gather(L_AG, l_all)
-
-    @pl.when(inner)
-    def _():
-        n_all[me] = total(N_RS, n_own[me], n_in).astype(BF)
+        n_all[me] = pair_total(N_RS, n_own, n_in).astype(BF)
         gather(N_AG, n_all)
 
     @pl.when(is_last)
     def _():
-        cross_scatter(L_RS, m_out, l_in, s - 1)
+        pair_send(M_PR, m_out, m_pair)
         load_rhs.wait()
-        base_field(range(blocks))
+        base_field(range(0, (blocks + 1) // 2))
+        pair_scatter(M_PR, M_RS, m_own, m_out, m_pair, m_in)
+        base_field(range((blocks + 1) // 2, blocks))
         split(dot(z[...], agg_b[...]), q_own, q_out)
         cross_row_scatter(R_RS, q_out, r_in, s - 1)
         du[...] = jnp.zeros_like(du)
+        m_all[me] = pair_total(M_RS, m_own, m_in).astype(BF)
+        every_leader(
+            lambda peer: remote(L_AG, m_all.at[me], l_all.at[me], s - 1, peer).start()
+        )
 
     @pl.when(is_direct)
     def _():
@@ -349,6 +381,8 @@
 
         load_dis_b.wait()
         back_matrix(range(blocks))
+        split_pairs(dot(u_b[...], agg_b[...]), n_own, n_out)
+        pair_send(N_PR, n_out, n_pair)
         load_agg.wait()
         shared(C_SH, c_all)
         cu[...] = dot(joined(c_all), u_f[...])
@@ -363,9 +397,8 @@
         cross_row_scatter(C_IN, b_out, c_in, s + 1)
         split(dot(rounded, agg_b[...]), q_own, q_out)
         row_scatter(Q_RS, q_out, q_in)
-        split(dot(u_b[...], agg_b[...]), n_own, n_out)
-        scatter(N_RS, n_out, n_in)
-        n_all[me] = total(N_RS, n_own[me], n_in).astype(BF)
+        pair_scatter(N_PR, N_RS, n_own, n_out, n_pair, n_in)
+        n_all[me] = pair_total(N_RS, n_own, n_in).astype(BF)
         gather(N_AG, n_all)
 
         @pl.when(leads)
@@ -401,7 +434,7 @@
         @pl.when(is_turn)
         def _():
             turned = cross_total(R_RS, r_in)
-            gathered(L_AG, l_all)
+            arrived(L_AG, l_all)
             d_all[slot] = (turned - dot(c_out[...], joined(l_all))).astype(BF)
 
         gathered(N_AG, n_all)
@@ -467,22 +500,18 @@
 
     @pl.when(inner)
     def _():
-        sent(T_RS, t_out.at[pl.ds(0, n - 1)])
-        sent(M_RS, m_out.at[pl.ds(0, n - 1)])
+        pair_sent(T_PR, T_RS, t_pair)
+        pair_sent(M_PR, M_RS, m_pair)
         by_role(sent, T_AG, t_all)
         by_role(sent, M_AG, m_all)
         by_role(sent, B_RS, b_out)
 
     @pl.when(between)
     def _():
-        sent(N_RS, n_out.at[pl.ds(0, n - 1)])
+        pair_sent(N_PR, N_RS, n_pair)
         by_role(sent, N_AG, n_all)
         by_role(sent, Q_RS, q_out)
 
-    @pl.when(is_turn)
-    def _():
-        by_role(sent, L_AG, l_all)
-
     @pl.when(jnp.logical_and(between, leads))
     def _():
         sent(C_SH, c_in.at[pl.ds(0, n - 1)])
@@ -502,7 +531,8 @@
 
     @pl.when(is_last)
     def _():
-        sent(L_RS, m_out)
+        pair_sent(M_PR, M_RS, m_pair)
+        sent(L_AG, m_all.at[pl.ds(0, leaders)])
         sent(R_RS, q_out)
 
 
@@ -532,7 +562,9 @@
             pltpu.VMEM((modes, unk), BF),
             pltpu.VMEM((modes, unk), BF),
         ]
-        + [pltpu.VMEM((n, part, modes), kind) for kind in (F32, BF, BF) * 3 + (BF,) * 5]
+        + [pltpu.VMEM((2, leaders, part, modes), kind) for kind in (F32,) * 3 + (BF,) * 3]
+        + [pltpu.VMEM((leaders, part, modes), BF)] * 6
+        + [pltpu.VMEM((n, part, modes), BF)] * 4
         + [
             pltpu.VMEM((count, rows, modes), kind)
             for count, kind in ((leaders, F32), (leaders, BF), (n, BF)) * 2 + ((n, BF),) * 2

time: 29.3 us -> 28.6 us (0.976)
  Pallas kernels: 27.5 us -> 26.8 us
    pallas_call x1, Pallas kernels: 27.5 us -> 26.8 us  [body(): pl.pallas_call(functools.partial(kernel, strips, n, width), out_shape=(ou...]
where the time goes in v5:
time: 28.6 us; the launch traced here: 28.4 us
  Pallas kernels  26.8 us (94%)
  other arithmetic  1 us (3%)
  between operations  0.64 us (2%)
    pallas_call x1, Pallas kernels, body(): pl.pallas_call(functools.partial(kernel, strips, n, width), out_shape=(ou...  26.8 us
    broadcast_in_dim x1, other arithmetic, body(): return (first[None], (first - du)[None])  1 us

profile of v5, /device:TPU:0, one launch (start us, length us, event | category | flops | bytes accessed | tf_op | source)
XLA Modules:
  0.0 28.4 jit_solution(9086618848089330367)
XLA Ops:
  0.6 26.8 %shard_map.113 = (f32[64,1792]{1,0:T(8,128)S(1)}, f32[64,1792]{1,0:T(8,128)S(1)}, f32[64,1792]{1,0:T(8,128)S(1)}) custom-call(bf16[1,64,1792]{2,1,0:T(8,128)(2,1)} %rhs.1, bf16[1,1,1792,1792]{3,2,1,0:T(8,128)(2,1)} %inverse.1, bf16[1,1,256,1792]{3,2,1,0:T(8,128)(2,1)} %dis_fwd.1, bf16[1,1792,256]{2,1,0:T(8,128)(2,1)} %agg_fwd.1, f32[1,128]{1,0:T(1,128)} %phase_fwd.1, ...), custom_call_target="tpu_custom_call" | custom-call | tf_op jit(solution)/shard_map/pallas_call | solution.py:549
  27.4 1.0 %subtract_bitcast_fusion = (f32[1,64,1792]{2,1,0:T(8,128)}, f32[1,64,1792]{2,1,0:T(8,128)}) fusion(f32[64,1792]{1,0:T(8,128)S(1)} %get-tuple-element.7, f32[64,1792]{1,0:T(8,128)S(1)} %get-tuple-element.5, f32[64,1792]{1,0:T(8,128)S(1)} %get-tuple-element.6), kind=kLoop, calls=%fused_computation | loop fusion | flops 229376 | bytes 2293760 | tf_op jit(solution)/shard_map/broadcast_in_dim | solution.py:580
